TPU v7x, 32 devices: a whole 2x2x4 slice. The times are simulated.
32 devices in a mesh: phys: 4 (over y, x), row: 2 (over core), col: 4 (over z).
Axes of the slice: x: 2, y: 2, z: 4, core: 2. Of those that a mesh axis runs over, the one named last changes fastest.
Arguments:
- rho_sites: bfloat16 [1, 16, 2048, 2048], P(None, 'phys', 'row', 'col'), may hold values from -0.0625 to 0.0625
- sigma_sites: bfloat16 [1, 16, 2048, 2048], P(None, 'phys', 'row', 'col'), may hold values from -0.0625 to 0.0625
- environment: float32 [2048, 2048], P('row', 'col'), may hold values from -6 to 6
Outputs:
- new_environment: float32 [2048, 2048], P('row', 'col')
All inputs are finite; a program needn't handle non-finite values.
Results may differ from a plain program's by a relative error of at most 0.004.
Values may be sent and summed in bfloat16 or wider, within the bound.
A program may use at most 128 MiB of HBM per device.

v0:
```python
import jax
import jax.numpy as jnp
from jax import lax
from jax.sharding import PartitionSpec as P


def per_device(rho_sites, sigma_sites, environment):
    env = environment
    rho_block = rho_sites[0]
    sigma_block = sigma_sites[0]
    env_b = env.astype(jnp.bfloat16)
    env_whole = lax.all_gather(env_b, "col", axis=1, tiled=True)
    half = jnp.einsum(
        "ik,pkl->pil",
        env_whole,
        lax.all_gather(sigma_block, "row", axis=1, tiled=True),
        preferred_element_type=jnp.float32,
    ).astype(jnp.bfloat16)
    partial_env = jnp.einsum(
        "pij,pil->jl",
        lax.all_gather(rho_block, "col", axis=2, tiled=True),
        half,
        preferred_element_type=jnp.float32,
    )
    row_part = lax.psum_scatter(partial_env, "row", scatter_dimension=0, tiled=True)
    env = lax.psum(row_part, "phys")
    return env


def solution(mesh):
    placed = (P(None, "phys", "row", "col"), P(None, "phys", "row", "col"), P("row", "col"))
    return jax.shard_map(
        per_device, mesh=mesh, in_specs=placed, out_specs=P("row", "col"), check_vma=False
    )
```

profile of v0, /device:TPU:0, one launch (start us, length us, event | category | flops | bytes accessed | tf_op | source)
XLA Modules:
  0.0 524.7 jit_solution(5357533425166158105)
XLA Ops:
  6.5 0.0 all-gather.6.cloned.1.call-start
  6.5 2.7 convert_element_type.9
  9.2 0.0 all-gather.6.cloned.1.call-update
  9.3 0.0 all-gather.8.cloned.1.call-start
  9.3 0.7 all-gather.8.cloned.1.call-update
  10.0 0.0 all-gather.10.cloned.1.call-start
  10.1 0.7 all-gather.10.cloned.1.call-update
  10.7 0.0 reduce-scatter.2.cloned.1.call-start
  10.8 82.1 %all-gather.6.cloned.1.call-done = bf16[1024,2048]{1,0:T(8,128)(2,1)} async-done(((bf16[1024,512]{1,0:T(8,128)(2,1)}), bf16[1024,2048]{1,0:T(8,128)(2,1)}) %all-gather.6.cloned.1.call-update) | async-done | bytes 4194320 | tf_op jit(solution)/shard_map/all_gather | solution.py:12
  92.9 19.9 %all-gather.8.cloned.1.call-done = bf16[1,4,2048,512]{3,2,1,0:T(8,128)(2,1)} async-done(((bf16[1,4,1024,512]{3,2,1,0:T(8,128)(2,1)}), bf16[1,4,2048,512]{3,2,1,0:T(8,128)(2,1)}) %all-gather.8.cloned.1.call-update) | async-done | bytes 8388624 | tf_op jit(solution)/shard_map/all_gather | solution.py:16
  112.8 289.5 %all-gather.10.cloned.1.call-done = bf16[1,4,1024,2048]{3,2,1,0:T(8,128)(2,1)} async-done(((bf16[1,4,1024,512]{3,2,1,0:T(8,128)(2,1)}), bf16[1,4,1024,2048]{3,2,1,0:T(8,128)(2,1)}) %all-gather.10.cloned.1.call-update) | async-done | bytes 16777232 | tf_op jit(solution)/shard_map/all_gather | solution.py:21
  402.3 29.0 %fusion.15 = f32[2048,512]{0,1:T(8,128)} fusion(bf16[1,4,1024,2048]{3,2,1,0:T(8,128)(2,1)} %all-gather.10.cloned.1.call-done, bf16[1024,2048]{1,0:T(8,128)(2,1)} %all-gather.6.cloned.1.call-done, bf16[1,4,2048,512]{3,2,1,0:T(8,128)(2,1)} %all-gather.8.cloned.1.call-done), kind=kOutput, calls=%fused_computation.7 | convolution fusion | flops 17181966336 | bytes 33554432 | tf_op jit(solution)/shard_map/pij,pil->jl/dot_general | solution.py:19
  431.3 0.0 reduce-scatter.2.cloned.1.call-update
  431.3 0.0 all-reduce.2.cloned.1.call-start
  431.4 10.2 %reduce-scatter.2.cloned.1.call-done = f32[1024,512]{0,1:T(8,128)} async-done(((f32[2048,512]{0,1:T(8,128)}), f32[1024,512]{0,1:T(8,128)}) %reduce-scatter.2.cloned.1.call-update) | async-done | bytes 2097168 | tf_op jit(solution)/shard_map/reduce_scatter | solution.py:25
  441.6 0.0 all-reduce.2.cloned.1.call-update
  441.6 73.7 %all-reduce.2.cloned.1.call-done = f32[1024,512]{0,1:T(8,128)} async-done(((f32[1024,512]{0,1:T(8,128)}), f32[1024,512]{0,1:T(8,128)}) %all-reduce.2.cloned.1.call-update) | async-done | bytes 2097168 | tf_op jit(solution)/shard_map/psum | solution.py:26
  515.3 2.9 copy.4
Async XLA Ops:
  6.5 86.3 %all-gather.6.cloned.1.call-start = ((), (), s32[]{:S(2)}) async-start(), calls=%async_computation.1 | async-start | bytes 5242880 | tf_op jit(solution)/shard_map/all_gather | solution.py:12
  9.3 103.5 %all-gather.8.cloned.1.call-start = ((), (), s32[]{:S(2)}) async-start(), calls=%async_computation.4 | async-start | bytes 12582912 | tf_op jit(solution)/shard_map/all_gather | solution.py:16
  10.0 392.3 %all-gather.10.cloned.1.call-start = ((), (), s32[]{:S(2)}) async-start(), calls=%async_computation.5 | async-start | bytes 20971520 | tf_op jit(solution)/shard_map/all_gather | solution.py:21
  10.7 430.8 %reduce-scatter.2.cloned.1.call-start = ((), (), s32[]{:S(2)}) async-start(), calls=%async_computation.2 | async-start | bytes 6291456 | tf_op jit(solution)/shard_map/reduce_scatter | solution.py:25
  431.3 84.0 %all-reduce.2.cloned.1.call-start = ((), (), s32[]{:S(2)}) async-start(), calls=%async_computation.3 | async-start | bytes 4194304 | tf_op jit(solution)/shard_map/psum | solution.py:26
Sparse Core Ops, SparseCore 0:
  9.4 83.4 all-gather.5
  94.4 18.3 all-gather.7
  114.4 287.9 all-gather.9
  431.5 10.0 reduce-scatter.1
  444.5 70.7 all-reduce.1
where the time goes:
time: 525 us
  waiting for transfers between devices  477 us (91%)
  matrix products  29 us (6%)
  between operations  13.1 us (2%)
    all_gather x1, waiting for transfers between devices, per_device(): lax.all_gather(rho_block, 'col', axis=2, tiled=True)  290 us
    all_gather x1, waiting for transfers between devices, per_device(): env_whole = lax.all_gather(env_b, 'col', axis=1, tiled=True)  82.1 us
    psum x1, waiting for transfers between devices, per_device(): env = lax.psum(row_part, 'phys')  73.7 us
    dot_general x1, matrix products, per_device(): jnp.einsum('pij,pil->jl', lax.all_gather(rho_block, 'col', axis=2, tiled=...  29 us
    all_gather x1, waiting for transfers between devices, per_device(): lax.all_gather(sigma_block, 'row', axis=1, tiled=True)  19.9 us
  transfers between devices with their start and end apart: 5, of which 5 were waited for; matrix products, arithmetic and copies ran while one was open for 0% of the time, Pallas kernels for 0%

commit v1 on v0

--- a/solution.py
+++ b/solution.py
@@ -23,7 +23,7 @@
         preferred_element_type=jnp.float32,
     )
     row_part = lax.psum_scatter(partial_env, "row", scatter_dimension=0, tiled=True)
-    env = lax.psum(row_part, "phys")
+    env = jnp.sum(lax.all_gather(row_part, "phys"), axis=0)
     return env
 
 

time: 525 us -> 560 us (1.067)
  waiting for transfers between devices: 477 us -> 494 us
  local copies, waits for them, and re-layouts: 2.88 us -> 12.6 us
  other arithmetic: 2.69 us -> 11.2 us
    all_gather x0 -> x1, waiting for transfers between devices: none -> 90.4 us  [per_device(): env = jnp.sum(lax.all_gather(row_part, 'phys'), axis=0)]
    psum x1 -> x0, waiting for transfers between devices: 73.7 us -> none  [per_device(): env = lax.psum(row_part, 'phys')]
    all_gather x0 -> x1, local copies, waits for them, and re-layouts: none -> 10.8 us  [per_device(): env = jnp.sum(lax.all_gather(row_part, 'phys'), axis=0)]
    reduce_sum x0 -> x1, other arithmetic: none -> 8.49 us  [per_device(): env = jnp.sum(lax.all_gather(row_part, 'phys'), axis=0)]
where the time goes in v1:
time: 560 us
  waiting for transfers between devices  494 us (88%)
  matrix products  29.2 us (5%)
  between operations  13.1 us (2%)
  local copies, waits for them, and re-layouts  12.6 us (2%)
  other arithmetic  11.2 us (2%)
    all_gather x1, waiting for transfers between devices, per_device(): lax.all_gather(rho_block, 'col', axis=2, tiled=True)  290 us
    all_gather x1, waiting for transfers between devices, per_device(): env = jnp.sum(lax.all_gather(row_part, 'phys'), axis=0)  90.4 us
    all_gather x1, waiting for transfers between devices, per_device(): env_whole = lax.all_gather(env_b, 'col', axis=1, tiled=True)  82.1 us
    dot_general x1, matrix products, per_device(): jnp.einsum('pij,pil->jl', lax.all_gather(rho_block, 'col', axis=2, tiled=...  29.2 us
    all_gather x1, waiting for transfers between devices, per_device(): lax.all_gather(sigma_block, 'row', axis=1, tiled=True)  19.9 us
  transfers between devices with their start and end apart: 5, of which 5 were waited for; matrix products, arithmetic and copies ran while one was open for 0% of the time, Pallas kernels for 0%

profile of v1, /device:TPU:0, one launch (start us, length us, event | category | flops | bytes accessed | tf_op | source)
XLA Modules:
  0.0 559.9 jit_solution(1895381589218193953)
XLA Ops:
  6.5 0.0 all-gather.8.cloned.1.call-start
  6.5 2.7 convert_element_type.9
  9.2 0.0 all-gather.8.cloned.1.call-update
  9.3 0.0 all-gather.10.cloned.1.call-start
  9.3 0.7 all-gather.10.cloned.1.call-update
  10.0 0.0 all-gather.12.cloned.1.call-start
  10.1 0.7 all-gather.12.cloned.1.call-update
  10.7 0.0 reduce-scatter.2.cloned.1.call-start
  10.8 82.1 %all-gather.8.cloned.1.call-done = bf16[1024,2048]{1,0:T(8,128)(2,1)} async-done(((bf16[1024,512]{1,0:T(8,128)(2,1)}), bf16[1024,2048]{1,0:T(8,128)(2,1)}) %all-gather.8.cloned.1.call-update) | async-done | bytes 4194320 | tf_op jit(solution)/shard_map/all_gather | solution.py:12
  92.9 19.9 %all-gather.10.cloned.1.call-done = bf16[1,4,2048,512]{3,2,1,0:T(8,128)(2,1)} async-done(((bf16[1,4,1024,512]{3,2,1,0:T(8,128)(2,1)}), bf16[1,4,2048,512]{3,2,1,0:T(8,128)(2,1)}) %all-gather.10.cloned.1.call-update) | async-done | bytes 8388624 | tf_op jit(solution)/shard_map/all_gather | solution.py:16
  112.8 289.5 %all-gather.12.cloned.1.call-done = bf16[1,4,1024,2048]{3,2,1,0:T(8,128)(2,1)} async-done(((bf16[1,4,1024,512]{3,2,1,0:T(8,128)(2,1)}), bf16[1,4,1024,2048]{3,2,1,0:T(8,128)(2,1)}) %all-gather.12.cloned.1.call-update) | async-done | bytes 16777232 | tf_op jit(solution)/shard_map/all_gather | solution.py:21
  402.3 29.2 %fusion.15 = f32[2048,512]{0,1:T(8,128)} fusion(bf16[1,4,1024,2048]{3,2,1,0:T(8,128)(2,1)} %all-gather.12.cloned.1.call-done, bf16[1024,2048]{1,0:T(8,128)(2,1)} %all-gather.8.cloned.1.call-done, bf16[1,4,2048,512]{3,2,1,0:T(8,128)(2,1)} %all-gather.10.cloned.1.call-done), kind=kOutput, calls=%fused_computation.7 | convolution fusion | flops 17181966336 | bytes 33554432 | tf_op jit(solution)/shard_map/pij,pil->jl/dot_general | solution.py:19
  431.5 0.0 reduce-scatter.2.cloned.1.call-update
  431.5 0.0 all-gather.14.cloned.1.call-start
  431.6 10.2 %reduce-scatter.2.cloned.1.call-done = f32[1024,512]{0,1:T(8,128)} async-done(((f32[2048,512]{0,1:T(8,128)}), f32[1024,512]{0,1:T(8,128)}) %reduce-scatter.2.cloned.1.call-update) | async-done | bytes 2097168 | tf_op jit(solution)/shard_map/reduce_scatter | solution.py:25
  441.8 0.0 all-gather.14.cloned.1.call-update
  441.8 90.4 %all-gather.14.cloned.1.call-done = f32[4096,512]{0,1:T(8,128)} async-done(((f32[1024,512]{0,1:T(8,128)}), f32[4096,512]{0,1:T(8,128)}) %all-gather.14.cloned.1.call-update) | async-done | bytes 8388624 | tf_op jit(solution)/shard_map/all_gather | solution.py:26
  532.2 10.8 %reshape.2 = f32[4,1024,512]{1,0,2:T(4,128)} reshape(f32[4096,512]{0,1:T(8,128)} %all-gather.14.cloned.1.call-done) | data formatting | bytes 16777216 | tf_op jit(solution)/shard_map/all_gather | solution.py:26
  543.0 8.5 %reduce_sum.9 = f32[1024,512]{0,1:T(8,128)S(1)} reduce(f32[4,1024,512]{1,0,2:T(4,128)} %reshape.2, f32[]{:T(128)} %constant.0.clone.1), dimensions={0}, to_apply=%region_1.0 | reduce | flops 1572864 | bytes 10485764 | tf_op jit(solution)/shard_map/reduce_sum | solution.py:26
  551.5 1.8 copy.4
Async XLA Ops:
  6.5 86.3 %all-gather.8.cloned.1.call-start = ((), (), s32[]{:S(2)}) async-start(), calls=%async_computation.1 | async-start | bytes 5242880 | tf_op jit(solution)/shard_map/all_gather | solution.py:12
  9.3 103.5 %all-gather.10.cloned.1.call-start = ((), (), s32[]{:S(2)}) async-start(), calls=%async_computation.3 | async-start | bytes 12582912 | tf_op jit(solution)/shard_map/all_gather | solution.py:16
  10.0 392.3 %all-gather.12.cloned.1.call-start = ((), (), s32[]{:S(2)}) async-start(), calls=%async_computation.4 | async-start | bytes 20971520 | tf_op jit(solution)/shard_map/all_gather | solution.py:21
  10.7 431.0 %reduce-scatter.2.cloned.1.call-start = ((), (), s32[]{:S(2)}) async-start(), calls=%async_computation.2 | async-start | bytes 6291456 | tf_op jit(solution)/shard_map/reduce_scatter | solution.py:25
  431.5 100.7 %all-gather.14.cloned.1.call-start = ((), (), s32[]{:S(2)}) async-start(), calls=%async_computation.5 | async-start | bytes 10485760 | tf_op jit(solution)/shard_map/all_gather | solution.py:26
Sparse Core Ops, SparseCore 0:
  9.4 83.4 all-gather.7
  94.4 18.3 all-gather.9
  114.4 287.9 all-gather.11
  431.7 10.0 reduce-scatter.1
  443.5 88.7 all-gather.13
